TPU v7x, 256 devices: a whole 4x4x8 slice. The times are simulated.
256 devices in a mesh: dp: 4 (over x), expert: 16 (over z, core), tp: 4 (over y).
Axes of the slice: x: 4, y: 4, z: 8, core: 2. Of those that a mesh axis runs over, the one named last changes fastest.
Arguments:
- hidden: bfloat16 [16, 64, 96, 5632], P('expert', 'dp', None, 'tp'), parts along dimension 1, may hold values from -6 to 6
- down_weight: bfloat16 [16, 5632, 3072], P('expert', 'tp'), may hold values from -0.078125 to 0.078125
- routes: int32 [16384, 4], P(('dp', 'expert')), parts along dimension 0, may hold values from 0 to 15, all different within a row; in each aligned block of 256 rows (0 to 255, 256 to 511, ...) at most 96 rows name the same one
- route_weight: float32 [16384, 4], P(('dp', 'expert')), parts along dimension 0, may hold values from 0.05 to 1
- residual: bfloat16 [16384, 3072], P(('dp', 'expert'), 'tp'), parts along dimension 0, may hold values from -6 to 6
Outputs:
- mixed: bfloat16 [16384, 3072], P(('dp', 'expert'), 'tp'), parts along dimension 0
There are 4 independent parts, one for each index of `dp`. A program takes and returns all parts, laid end to end along the dimension named above; an argument that names none is the same for every part. Nothing has to cross between parts.
Inputs may be any that keep to these rules, and one draw needn't show every extreme that they name: `routes`: each row names 4 different experts. Among the 256 rows of one source group no expert is named by more than 96 rows, a bound that some of them reach.
All inputs are finite; a program needn't handle non-finite values.
Results may differ from a plain program's by a relative error of at most 0.0095.
Values may be sent and summed in bfloat16 or wider, within the bound.
A program may use at most 128 MiB of HBM per device.

v0:
```python
import jax
import jax.numpy as jnp
from jax import lax
from jax.sharding import PartitionSpec as P

EXPERTS = 16


def slot_table(routes):
    expert_ids = jnp.arange(EXPERTS, dtype=jnp.int32)
    matches = (routes[:, :, None] == expert_ids[None, None, :]).astype(jnp.int32)
    onehot = jnp.sum(matches, axis=1)
    before = jnp.cumsum(onehot, axis=0) - onehot
    return jnp.sum(matches * before[:, None, :], axis=2)


def combine(received, routes, route_weight, slot_of):
    capacity = received.shape[1]
    width = received.shape[2]
    flattened = received.reshape(-1, width)
    slot_index = (routes * capacity + slot_of).reshape(-1)
    picked = (
        flattened[slot_index].astype(jnp.float32).reshape(routes.shape[0], routes.shape[1], width)
    )
    share = route_weight / jnp.sum(route_weight, axis=1, keepdims=True)
    return jnp.sum(share[:, :, None] * picked, axis=1)


def on_device(hidden, down_weight, routes, route_weight, residual):
    slot_of = slot_table(routes)
    partial_value = jnp.einsum(
        "lsch,lhd->slcd", hidden, down_weight, preferred_element_type=jnp.float32
    ).astype(jnp.bfloat16)
    received = lax.all_to_all(partial_value, "expert", split_axis=0, concat_axis=1, tiled=True)
    mixed_part = combine(received[0], routes, route_weight, slot_of)
    expert_mix = lax.psum_scatter(
        mixed_part.astype(jnp.bfloat16), "tp", scatter_dimension=1, tiled=True
    ).astype(jnp.float32)
    return (residual.astype(jnp.float32) + expert_mix).astype(jnp.bfloat16)


def solution(mesh):
    return jax.shard_map(
        on_device,
        mesh=mesh,
        in_specs=(
            P("expert", "dp", None, "tp"),
            P("expert", "tp", None),
            P(("dp", "expert"), None),
            P(("dp", "expert"), None),
            P(("dp", "expert"), "tp"),
        ),
        out_specs=P(("dp", "expert"), "tp"),
        check_vma=False,
    )
```

profile of v0, /device:TPU:2, one launch (start us, length us, event | category | flops | bytes accessed | tf_op | source)
XLA Modules:
  0.0 319.9 jit_solution(6353277664045412335)
XLA Ops:
  6.5 20.0 %convert_bitcast_fusion = bf16[16,1,96,3072]{3,2,1,0:T(8,128)(2,1)} fusion(bf16[1,1408,3072]{2,1,0:T(8,128)(2,1)} %param.6, bf16[1,16,96,1408]{3,2,1,0:T(8,128)(2,1)} %param.5), kind=kOutput, calls=%fused_computation.2 | convolution fusion | flops 13292273664 | bytes 22413312 | tf_op jit(solution)/shard_map/lsch,lhd->slcd/dot_general | solution.py:31
  26.5 0.0 copy-start.1
  26.5 0.0 copy-start.2
  26.5 8.8 %all-to-all-start = ((bf16[16,1,96,3072]{3,2,1,0:T(8,128)(2,1)}), bf16[16,1,96,3072]{3,2,1,0:T(8,128)(2,1)}, u32[]{:S(2)}, u32[]{:S(2)}) async-start(bf16[16,1,96,3072]{3,2,1,0:T(8,128)(2,1)} %convert_bitcast_fusion), calls=%async_computation | async-start | bytes 18874368 | tf_op jit(solution)/shard_map/all_to_all | solution.py:34
  35.3 0.0 reduce-scatter.2.cloned.1.call-start
  35.3 0.0 copy-done.1
  35.3 0.6 reduce-window.6
  35.9 0.2 slice_reduce_fusion
  36.2 0.1 fusion.5
  36.3 0.1 copy.25
  36.4 0.1 reshape.65
  36.5 0.0 copy-done.2
  36.6 0.1 copy.21
  36.8 205.1 %all-to-all-done = bf16[16,1,96,3072]{3,2,1,0:T(8,128)(2,1)} async-done(((bf16[16,1,96,3072]{3,2,1,0:T(8,128)(2,1)}), bf16[16,1,96,3072]{3,2,1,0:T(8,128)(2,1)}, u32[]{:S(2)}, u32[]{:S(2)}) %all-to-all-start) | async-done | bytes 9437216 | tf_op jit(solution)/shard_map/all_to_all | solution.py:34
  241.9 17.1 %gather_fusion = bf16[1024,3072]{1,0:T(8,128)(2,1)} fusion(bf16[1536,3072]{1,0:T(8,128)(2,1)} %bitcast.6, s32[1024]{0:T(1024)S(1)} %broadcast_clamp_fusion), kind=kCustom, calls=%fused_computation | custom fusion | bytes 12587008 | tf_op jit(solution)/shard_map/gather | solution.py:23
  259.0 12.2 %reshape.66 = f32[256,4,3072]{2,1,0:T(4,128)} reshape(bf16[1024,3072]{1,0:T(8,128)(2,1)} %gather_fusion) | data formatting | bytes 18874368 | tf_op jit(solution)/shard_map/convert_element_type | solution.py:23
  271.3 0.0 copy-start
  271.3 12.2 %multiply_reduce_fusion = bf16[256,3072]{1,0:T(8,128)(2,1)} fusion(f32[256,4,3072]{2,1,0:T(4,128)} %reshape.66, f32[256,4]{1,0:T(8,128)S(1)} %copy.21), kind=kLoop, calls=%fused_computation.1 | loop fusion | flops 5505024 | bytes 14159872 | tf_op jit(solution)/shard_map/reduce_sum | solution.py:26
  283.5 0.0 reduce-scatter.2.cloned.1.call-update
  283.5 27.7 %reduce-scatter.2.cloned.1.call-done = bf16[256,768]{1,0:T(8,128)(2,1)} async-done(((bf16[256,3072]{1,0:T(8,128)(2,1)}), bf16[256,768]{1,0:T(8,128)(2,1)}) %reduce-scatter.2.cloned.1.call-update) | async-done | bytes 393232 | tf_op jit(solution)/shard_map/reduce_scatter | solution.py:36
  311.2 0.0 copy-done
  311.2 1.8 add_convert_fusion
  (10 shorter events, 0.1 us)
Async XLA Ops:
  26.5 8.8 %copy-start.1 = (s32[256,4]{0,1:T(4,128)S(1)}, s32[256,4]{0,1:T(4,128)}, u32[]{:S(2)}) copy-start(s32[256,4]{0,1:T(4,128)} %param.7) | copy-start | bytes 12292
  26.5 10.1 %copy-start.2 = (f32[256,4]{0,1:T(4,128)S(1)}, f32[256,4]{0,1:T(4,128)}, u32[]{:S(2)}) copy-start(f32[256,4]{0,1:T(4,128)} %param.8) | copy-start | bytes 12292
  26.5 215.4 %all-to-all-start = ((bf16[16,1,96,3072]{3,2,1,0:T(8,128)(2,1)}), bf16[16,1,96,3072]{3,2,1,0:T(8,128)(2,1)}, u32[]{:S(2)}, u32[]{:S(2)}) async-start(bf16[16,1,96,3072]{3,2,1,0:T(8,128)(2,1)} %convert_bitcast_fusion), calls=%async_computation | async-start | bytes 18874368 | tf_op jit(solution)/shard_map/all_to_all | solution.py:34
  35.3 275.9 %reduce-scatter.2.cloned.1.call-start = ((), (), s32[]{:S(2)}) async-start(), calls=%async_computation.2 | async-start | bytes 1966080 | tf_op jit(solution)/shard_map/reduce_scatter | solution.py:36
  271.3 39.9 %copy-start = (bf16[256,768]{1,0:T(8,128)(2,1)S(1)}, bf16[256,768]{1,0:T(8,128)(2,1)}, u32[]{:S(2)}) copy-start(bf16[256,768]{1,0:T(8,128)(2,1)} %param.9) | copy-start | bytes 1179652
Sparse Core Ops, SparseCore 0:
  283.6 27.4 reduce-scatter.1
where the time goes:
time: 320 us
  waiting for transfers between devices  233 us (73%)
  local copies, waits for them, and re-layouts  30 us (9%)
  matrix products  20 us (6%)
  other arithmetic  14.9 us (5%)
  between operations  13.5 us (4%)
  starting transfers between devices  8.79 us (3%)
    all_to_all x1, waiting for transfers between devices, on_device(): lax.all_to_all(partial_value, 'expert', split_axis=0, concat_axis=1, tile...  205 us
    reduce_scatter x1, waiting for transfers between devices, on_device(): lax.psum_scatter(mixed_part.astype(jnp.bfloat16), 'tp', scatter_dimension...  27.7 us
    dot_general x1, matrix products, on_device(): jnp.einsum('lsch,lhd->slcd', hidden, down_weight, preferred_element_type=...  20 us
    gather x1, local copies, waits for them, and re-layouts, combine(): flattened[slot_index].astype(jnp.float32)  17.1 us
    reduce_sum x1, other arithmetic, combine(): return jnp.sum(share[:, :, None] * picked, axis=1)  12.2 us
    convert_element_type x1, local copies, waits for them, and re-layouts, combine(): flattened[slot_index].astype(jnp.float32)  12.2 us
    all_to_all x1, starting transfers between devices, on_device(): lax.all_to_all(partial_value, 'expert', split_axis=0, concat_axis=1, tile...  8.75 us
  transfers between devices with their start and end apart: 2, of which 2 were waited for; matrix products, arithmetic and copies ran while one was open for 0% of the time, Pallas kernels for 0%

commit v1 on v0

--- a/solution.py
+++ b/solution.py
@@ -31,7 +31,12 @@
     partial_value = jnp.einsum(
         "lsch,lhd->slcd", hidden, down_weight, preferred_element_type=jnp.float32
     ).astype(jnp.bfloat16)
-    received = lax.all_to_all(partial_value, "expert", split_axis=0, concat_axis=1, tiled=True)
+    received = jnp.concatenate(
+        lax.all_to_all(
+            jnp.stack(jnp.split(partial_value, lax.axis_size("expert"), axis=0)), "expert", 0, 0
+        ),
+        axis=1,
+    )
     mixed_part = combine(received[0], routes, route_weight, slot_of)
     expert_mix = lax.psum_scatter(
         mixed_part.astype(jnp.bfloat16), "tp", scatter_dimension=1, tiled=True

time: 320 us -> 333 us (1.041)
  local copies, waits for them, and re-layouts: 30 us -> 43.8 us
    unnamed x6 -> x21, local copies, waits for them, and re-layouts: 0.01 us -> 13 us
where the time goes in v1:
time: 333 us; the launch traced here: 332 us
  waiting for transfers between devices  233 us (70%)
  local copies, waits for them, and re-layouts  43.8 us (13%)
  matrix products  18.3 us (5%)
  other arithmetic  14.9 us (4%)
  between operations  13.5 us (4%)
  starting transfers between devices  8.97 us (3%)
    all_to_all x1, waiting for transfers between devices, on_device(): lax.all_to_all(jnp.stack(jnp.split(partial_value, lax.axis_size('expert')...  205 us
    reduce_scatter x1, waiting for transfers between devices, on_device(): lax.psum_scatter(mixed_part.astype(jnp.bfloat16), 'tp', scatter_dimension...  27.7 us
    dot_general x1, matrix products, on_device(): jnp.einsum('lsch,lhd->slcd', hidden, down_weight, preferred_element_type=...  18.3 us
    gather x1, local copies, waits for them, and re-layouts, combine(): flattened[slot_index].astype(jnp.float32)  17.1 us
    unnamed x21, local copies, waits for them, and re-layouts  13 us
    reduce_sum x1, other arithmetic, combine(): return jnp.sum(share[:, :, None] * picked, axis=1)  12.2 us
    convert_element_type x1, local copies, waits for them, and re-layouts, combine(): flattened[slot_index].astype(jnp.float32)  12.2 us
    all_to_all x1, starting transfers between devices, on_device(): lax.all_to_all(jnp.stack(jnp.split(partial_value, lax.axis_size('expert')...  8.75 us
  transfers between devices with their start and end apart: 2, of which 2 were waited for; matrix products, arithmetic and copies ran while one was open for 0% of the time, Pallas kernels for 0%

profile of v1, /device:TPU:2, one launch (start us, length us, event | category | flops | bytes accessed | tf_op | source)
XLA Modules:
  0.0 332.1 jit_solution(7942111441979342796)
XLA Ops:
  6.5 18.3 %fusion.2 = bf16[3072,16,96]{0,2,1:T(8,128)(2,1)S(1)} fusion(bf16[1,1408,3072]{2,1,0:T(8,128)(2,1)} %param.6, bf16[1,16,96,1408]{3,2,1,0:T(8,128)(2,1)} %param.5), kind=kOutput, calls=%fused_computation.4 | convolution fusion | flops 13292273664 | bytes 22413312 | tf_op jit(solution)/shard_map/lsch,lhd->slcd/dot_general | solution.py:31
  24.8 0.8 fusion.21
  25.7 0.8 fusion.20
  26.5 0.9 fusion.19
  27.4 0.9 fusion.18
  28.3 0.9 fusion.17
  29.1 0.9 fusion.16
  30.0 0.9 fusion.15
  30.9 0.8 fusion.14
  31.7 0.8 fusion.13
  32.6 0.9 fusion.12
  33.5 0.9 fusion.11
  34.3 0.9 fusion.10
  35.2 0.9 fusion.9
  36.1 0.9 fusion.8
  37.0 0.9 fusion.7
  37.8 0.9 fusion.6
  38.7 0.0 copy-start.1
  38.7 0.0 copy-start.2
  38.7 8.7 %all-to-all-start = ((bf16[16,1,1,96,3072]{4,3,2,1,0:T(8,128)(2,1)}), bf16[16,1,1,96,3072]{4,3,2,1,0:T(8,128)(2,1)}, u32[]{:S(2)}, u32[]{:S(2)}) async-start(bf16[16,1,1,96,3072]{4,3,2,1,0:T(8,128)(2,1)} %fusion.6), calls=%async_computation | async-start | bytes 18874368 | tf_op jit(solution)/shard_map/all_to_all | solution.py:35
  47.5 0.2 reduce-scatter.2.cloned.1.call-start
  47.7 0.0 copy-done.1
  47.7 0.6 reduce-window.6
  48.3 0.2 slice_reduce_fusion
  48.5 0.1 fusion.22
  48.7 0.1 copy.62
  48.8 0.1 reshape.61
  48.9 0.0 copy-done.2
  49.0 0.1 copy.44
  49.2 204.9 %all-to-all-done = bf16[16,1,1,96,3072]{4,3,2,1,0:T(8,128)(2,1)} async-done(((bf16[16,1,1,96,3072]{4,3,2,1,0:T(8,128)(2,1)}), bf16[16,1,1,96,3072]{4,3,2,1,0:T(8,128)(2,1)}, u32[]{:S(2)}, u32[]{:S(2)}) %all-to-all-start) | async-done | bytes 9437216 | tf_op jit(solution)/shard_map/all_to_all | solution.py:35
  254.1 17.1 %gather_fusion = bf16[1024,3072]{1,0:T(8,128)(2,1)} fusion(bf16[1536,3072]{1,0:T(8,128)(2,1)} %bitcast.37, s32[1024]{0:T(1024)S(1)} %broadcast_clamp_fusion), kind=kCustom, calls=%fused_computation | custom fusion | bytes 12587008 | tf_op jit(solution)/shard_map/gather | solution.py:23
  271.2 12.2 %reshape.62 = f32[256,4,3072]{2,1,0:T(4,128)} reshape(bf16[1024,3072]{1,0:T(8,128)(2,1)} %gather_fusion) | data formatting | bytes 18874368 | tf_op jit(solution)/shard_map/convert_element_type | solution.py:23
  283.5 0.0 copy-start
  283.5 12.2 %multiply_reduce_fusion = bf16[256,3072]{1,0:T(8,128)(2,1)} fusion(f32[256,4,3072]{2,1,0:T(4,128)} %reshape.62, f32[256,4]{1,0:T(8,128)S(1)} %copy.44), kind=kLoop, calls=%fused_computation.1 | loop fusion | flops 5505024 | bytes 14159872 | tf_op jit(solution)/shard_map/reduce_sum | solution.py:26
  295.7 0.0 reduce-scatter.2.cloned.1.call-update
  295.7 27.7 %reduce-scatter.2.cloned.1.call-done = bf16[256,768]{1,0:T(8,128)(2,1)} async-done(((bf16[256,3072]{1,0:T(8,128)(2,1)}), bf16[256,768]{1,0:T(8,128)(2,1)}) %reduce-scatter.2.cloned.1.call-update) | async-done | bytes 393232 | tf_op jit(solution)/shard_map/reduce_scatter | solution.py:41
  323.4 0.0 copy-done
  323.4 1.8 add_convert_fusion
  (10 shorter events, 0.1 us)
Async XLA Ops:
  38.7 9.0 %copy-start.1 = (s32[256,4]{0,1:T(4,128)S(1)}, s32[256,4]{0,1:T(4,128)}, u32[]{:S(2)}) copy-start(s32[256,4]{0,1:T(4,128)} %param.7) | copy-start | bytes 12292
  38.7 10.2 %copy-start.2 = (f32[256,4]{0,1:T(4,128)S(1)}, f32[256,4]{0,1:T(4,128)}, u32[]{:S(2)}) copy-start(f32[256,4]{0,1:T(4,128)} %param.8) | copy-start | bytes 12292
  38.7 215.4 %all-to-all-start = ((bf16[16,1,1,96,3072]{4,3,2,1,0:T(8,128)(2,1)}), bf16[16,1,1,96,3072]{4,3,2,1,0:T(8,128)(2,1)}, u32[]{:S(2)}, u32[]{:S(2)}) async-start(bf16[16,1,1,96,3072]{4,3,2,1,0:T(8,128)(2,1)} %fusion.6), calls=%async_computation | async-start | bytes 18874368 | tf_op jit(solution)/shard_map/all_to_all | solution.py:35
  47.5 275.9 %reduce-scatter.2.cloned.1.call-start = ((), (), s32[]{:S(2)}) async-start(), calls=%async_computation.2 | async-start | bytes 1966080 | tf_op jit(solution)/shard_map/reduce_scatter | solution.py:41
  283.5 39.9 %copy-start = (bf16[256,768]{1,0:T(8,128)(2,1)S(1)}, bf16[256,768]{1,0:T(8,128)(2,1)}, u32[]{:S(2)}) copy-start(bf16[256,768]{1,0:T(8,128)(2,1)} %param.9) | copy-start | bytes 1179652
Sparse Core Ops, SparseCore 0:
  295.8 27.4 reduce-scatter.1
